TPU v7x, 128 devices: a whole 4x4x4 slice. The times are simulated.
128 devices in a mesh: range: 16 (over z, y), doppler: 8 (over x, core).
Axes of the slice: x: 4, y: 4, z: 4, core: 2. Of those that a mesh axis runs over, the one named last changes fastest.
Arguments:
- snapshots: bfloat16 [128, 16384, 384], P(None, ('range', 'doppler')), may hold values from -24 to 24
- steering: bfloat16 [128, 384, 256], P(('range', 'doppler')), may hold values from -0.3125 to 0.3125
- train_list: int32 [128, 128], P(('range', 'doppler')), may hold values from 0 to 127, each once within a row
- train_count: int32 [128], P(('range', 'doppler')), may hold values from 42 to 128, as said below
Outputs:
- beam_output: bfloat16 [128, 16384, 256], P(None, ('range', 'doppler'))
Inputs may be any that keep to these rules, and one draw needn't show every extreme that they name: `train_count`: some bin trains on all 128 blocks and some bin on 42.
All inputs are finite; a program needn't handle non-finite values.
Results may differ from a plain program's by a relative error of at most 0.0052.
Values may be sent and summed in bfloat16 or wider, within the bound.
A program may use at most 128 MiB of HBM per device.

v0:
```python
import jax
import jax.numpy as jnp
from jax import lax
from jax.sharding import PartitionSpec as P

BLOCK = 128
LOADING = 0.1


def selection(train_list, train_count):
    block_total = train_list.shape[1]
    position = lax.broadcasted_iota(jnp.int32, (1, block_total, 1), 1)
    block_ids = lax.broadcasted_iota(jnp.int32, (1, 1, block_total), 2)
    matches = (train_list[:, :, None] == block_ids) & (position < train_count[:, None, None])
    return jnp.sum(matches.astype(jnp.int32), axis=1)


def solve_one(factor, rhs_block):
    inner = lax.linalg.triangular_solve(factor, rhs_block, left_side=True, lower=True)
    return lax.linalg.triangular_solve(factor, inner, left_side=True, lower=True, transpose_a=True)


def adapt(own_snaps, train_list, train_count, steering):
    own_bins, gate_total, channels = own_snaps.shape
    block_total = train_list.shape[1]
    chosen = selection(train_list, train_count)
    blocks = own_snaps.reshape(own_bins, block_total, gate_total // block_total, channels)
    masked = blocks * chosen.astype(own_snaps.dtype)[:, :, None, None]
    gram_sum = jnp.einsum("bnrd,bnre->bde", masked, blocks, preferred_element_type=jnp.float32)
    scale = (BLOCK * train_count).astype(jnp.float32)
    covariance = (
        gram_sum / scale[:, None, None] + LOADING * jnp.eye(channels, dtype=jnp.float32)[None]
    )
    factor = jnp.linalg.cholesky(covariance)
    steer_full = steering.astype(jnp.float32)
    solved = jax.vmap(solve_one)(factor, steer_full)
    response = jnp.sum(steer_full * solved, axis=1)
    return (solved / response[:, None, :]).astype(jnp.bfloat16)


def body(snapshots, steering, train_list, train_count):
    bin_total, gate_rows, channels = snapshots.shape
    own_bins = steering.shape[0]
    devices = bin_total // own_bins
    outgoing = snapshots.reshape(devices, own_bins, gate_rows, channels)
    arrived = lax.all_to_all(
        outgoing, ("range", "doppler"), split_axis=0, concat_axis=0, tiled=True
    )
    own_snaps = jnp.moveaxis(arrived, 1, 0).reshape(own_bins, devices * gate_rows, channels)
    weights = adapt(own_snaps, train_list, train_count, steering)
    return jnp.einsum(
        "bgd,bde->bge",
        snapshots,
        lax.all_gather(weights, ("range", "doppler"), axis=0, tiled=True),
        preferred_element_type=jnp.float32,
    ).astype(jnp.bfloat16)


def solution(mesh):
    placed = (
        P(None, ("range", "doppler"), None),
        P(("range", "doppler"), None, None),
        P(("range", "doppler"), None),
        P(("range", "doppler")),
    )
    return jax.shard_map(
        body,
        mesh=mesh,
        in_specs=placed,
        out_specs=P(None, ("range", "doppler"), None),
        check_vma=False,
    )
```

profile of v0, /device:TPU:1, one launch (start us, length us, event | category | flops | bytes accessed | tf_op | source)
XLA Modules:
  0.0 431.1 jit_solution(15140216038816594535)
XLA Ops:
  6.5 11.9 %all-to-all-start = ((bf16[128,1,128,384]{3,2,1,0:T(8,128)(2,1)}), bf16[128,1,128,384]{3,2,1,0:T(8,128)(2,1)}, u32[]{:S(2)}, u32[]{:S(2)}) async-start(bf16[128,1,128,384]{3,2,1,0:T(8,128)(2,1)} %bitcast.154), calls=%async_computation | async-start | bytes 25165824 | tf_op jit(solution)/shard_map/all_to_all | solution.py:46
  19.4 150.7 %all-to-all-done = bf16[128,1,128,384]{3,2,1,0:T(8,128)(2,1)} async-done(((bf16[128,1,128,384]{3,2,1,0:T(8,128)(2,1)}), bf16[128,1,128,384]{3,2,1,0:T(8,128)(2,1)}, u32[]{:S(2)}, u32[]{:S(2)}) %all-to-all-start) | async-done | bytes 12582944 | tf_op jit(solution)/shard_map/all_to_all | solution.py:46
  170.0 14.2 %fusion.22 = f32[384,384]{0,1:T(8,128)S(1)} fusion(bf16[128,1,128,384]{3,2,1,0:T(8,128)(2,1)} %all-to-all-done, bf16[128]{0:T(256)(128)(2,1)S(1)} %convert_element_type.45, f32[]{:T(128)} %bitcast.6), kind=kOutput, calls=%fused_computation.26 | convolution fusion | flops 4838719488 | bytes 13172996 | tf_op jit(solution)/shard_map/bnrd,bnre->bde/dot_general | solution.py:29
  184.5 11.7 %custom-call.27 = f32[1,128,128]{2,1,0:T(8,128)S(1)} custom-call(f32[1,128,128]{2,1,0:T(8,128)S(1)} %cholesky.192), custom_call_target="Cholesky" | custom-call | tf_op jit(solution)/shard_map/jit(cholesky)/cholesky | solution.py:34
  196.3 9.8 %custom-call.28 = f32[1,1,128,128]{2,3,1,0:T(8,128)S(1)} custom-call(f32[1,1,128,128]{3,2,1,0:T(8,128)S(1)} %get-tuple-element.29), custom_call_target="InvertDiagBlocksLowerTriangular" | custom-call | tf_op jit(solution)/shard_map/jit(cholesky)/cholesky | solution.py:34
  206.7 11.7 %custom-call.29 = f32[1,128,128]{2,1,0:T(8,128)S(1)} custom-call(f32[1,128,128]{2,1,0:T(8,128)S(1)} %cholesky.196), custom_call_target="Cholesky" | custom-call | tf_op jit(solution)/shard_map/jit(cholesky)/cholesky | solution.py:34
  218.4 10.0 %custom-call.30 = f32[1,1,128,128]{2,3,1,0:T(8,128)S(1)} custom-call(f32[1,1,128,128]{3,2,1,0:T(8,128)S(1)} %get-tuple-element.26), custom_call_target="InvertDiagBlocksLowerTriangular" | custom-call | tf_op jit(solution)/shard_map/jit(cholesky)/cholesky | solution.py:34
  228.9 11.7 %custom-call.31 = f32[1,128,128]{2,1,0:T(8,128)S(1)} custom-call(f32[1,128,128]{2,1,0:T(8,128)S(1)} %fusion.16), custom_call_target="Cholesky" | custom-call | tf_op jit(solution)/shard_map/jit(cholesky)/cholesky | solution.py:34
  240.7 0.7 compare_reduce_fusion
  241.4 0.7 compare_reduce_fusion.1
  244.0 6.1 %while.1 = (s32[]{:T(128)}, f32[1,384,384]{2,1,0:T(8,128)S(1)}, s32[3,2]{0,1:T(2,128)S(1)}, f32[3,1,128,128]{3,2,1,0:T(8,128)S(1)}, s32[]{:T(128)}) while((s32[]{:T(128)}, f32[1,384,384]{2,1,0:T(8,128)S(1)}, s32[3,2]{0,1:T(2,128)S(1)}, f32[3,1,128,128]{3,2,1,0:T(8,128)S(1)}, s32[]{:T(128)}) %tuple.25), condition=%wide.while_cond, body=%wide.while_body.sunk | while | flops 2 | bytes 131189 | solution.py:20
  244.1 0.6 fusion.56
  244.7 1.3 bitcast_dynamic-update-slice_fusion.2
  246.2 0.6 fusion.56
  246.8 1.3 bitcast_dynamic-update-slice_fusion.2
  248.2 0.6 fusion.56
  248.8 1.3 bitcast_dynamic-update-slice_fusion.2
  250.1 29.5 %custom-call.32 = f32[1,3,128,128]{2,3,1,0:T(8,128)S(1)} custom-call(f32[1,3,128,128]{3,2,1,0:T(8,128)S(1)} %bitcast.162), custom_call_target="InvertDiagBlocksLowerTriangular" | custom-call | tf_op jit(solution)/shard_map/vmap()/triangular_solve | solution.py:20
  281.4 0.3 convolution_subtract_fusion.1
  282.0 0.4 convolution_subtract_fusion
  282.7 0.7 divide_convert_fusion
  283.5 110.9 %all-gather.2.cloned.1.call-done = bf16[128,384,256]{2,1,0:T(8,128)(2,1)} async-done(((bf16[1,384,256]{2,1,0:T(8,128)(2,1)}), bf16[128,384,256]{2,1,0:T(8,128)(2,1)}) %all-gather.2.cloned.1.call-update) | async-done | bytes 25165840 | tf_op jit(solution)/shard_map/all_gather | solution.py:54
  394.4 18.0 %convert_bitcast_fusion = bf16[128,128,256]{1,2,0:T(8,128)(2,1)} fusion(bf16[128,384,256]{2,1,0:T(8,128)(2,1)} %all-gather.2.cloned.1.call-done, bf16[128,128,384]{2,1,0:T(8,128)(2,1)} %param.4), kind=kOutput, calls=%fused_computation.6 | convolution fusion | flops 3225419776 | bytes 46137344 | tf_op jit(solution)/shard_map/bgd,bde->bge/dot_general | solution.py:51
  412.4 11.9 %copy.19 = bf16[128,128,256]{2,1,0:T(8,128)(2,1)} copy(bf16[128,128,256]{1,2,0:T(8,128)(2,1)} %convert_bitcast_fusion) | data formatting | bytes 16777216 | tf_op jit(solution)/shard_map/convert_element_type | solution.py:56
  (38 shorter events, 4.3 us)
Async XLA Ops:
  6.5 12.6 %copy-start.1 = (s32[1,128]{1,0:T(1,128)S(1)}, s32[1,128]{1,0:T(1,128)}, u32[]{:S(2)}) copy-start(s32[1,128]{1,0:T(1,128)} %param.6) | copy-start | bytes 1540
  6.5 12.8 %copy-start = (bf16[1,384,256]{2,1,0:T(8,128)(2,1)S(1)}, bf16[1,384,256]{2,1,0:T(8,128)(2,1)}, u32[]{:S(2)}) copy-start(bf16[1,384,256]{2,1,0:T(8,128)(2,1)} %param.5) | copy-start | bytes 589828
  6.5 163.5 %all-to-all-start = ((bf16[128,1,128,384]{3,2,1,0:T(8,128)(2,1)}), bf16[128,1,128,384]{3,2,1,0:T(8,128)(2,1)}, u32[]{:S(2)}, u32[]{:S(2)}) async-start(bf16[128,1,128,384]{3,2,1,0:T(8,128)(2,1)} %bitcast.154), calls=%async_computation | async-start | bytes 25165824 | tf_op jit(solution)/shard_map/all_to_all | solution.py:46
  18.4 375.9 %all-gather.2.cloned.1.call-start = ((), (), s32[]{:S(2)}) async-start(), calls=%async_computation.1 | async-start | bytes 25362432 | tf_op jit(solution)/shard_map/all_gather | solution.py:54
Sparse Core Ops, SparseCore 0:
  283.6 110.7 all-gather.1
where the time goes:
time: 432 us; the launch traced here: 431 us
  waiting for transfers between devices  262 us (61%)
  other arithmetic  87 us (20%)
  matrix products  36.1 us (8%)
  local copies, waits for them, and re-layouts  18.2 us (4%)
  between operations  16.2 us (4%)
  starting transfers between devices  11.9 us (3%)
    all_to_all x1, waiting for transfers between devices, body(): lax.all_to_all(outgoing, ('range', 'doppler'), split_axis=0, concat_axis=...  151 us
    all_gather x1, waiting for transfers between devices, body(): lax.all_gather(weights, ('range', 'doppler'), axis=0, tiled=True)  111 us
    another operation x10, other arithmetic, adapt(): factor = jnp.linalg.cholesky(covariance)  56.4 us
    another operation x3, other arithmetic, solve_one(): lax.linalg.triangular_solve(factor, inner, left_side=True, lower=True, tr...  29.5 us
    dot_general x1, matrix products, body(): jnp.einsum('bgd,bde->bge', snapshots, lax.all_gather(weights, ('range', '...  18 us
    dot_general x1, matrix products, adapt(): jnp.einsum('bnrd,bnre->bde', masked, blocks, preferred_element_type=jnp.f...  14.2 us
    convert_element_type x1, local copies, waits for them, and re-layouts, body(): return jnp.einsum('bgd,bde->bge', snapshots, lax.all_gather(weights, ('ra...  11.9 us
    all_to_all x1, starting transfers between devices, body(): lax.all_to_all(outgoing, ('range', 'doppler'), split_axis=0, concat_axis=...  11.9 us
  transfers between devices with their start and end apart: 2, of which 2 were waited for; matrix products, arithmetic and copies ran while one was open for 0% of the time, Pallas kernels for 0%

commit v1 on v0

--- a/solution.py
+++ b/solution.py
@@ -51,7 +51,15 @@
     return jnp.einsum(
         "bgd,bde->bge",
         snapshots,
-        lax.all_gather(weights, ("range", "doppler"), axis=0, tiled=True),
+        jnp.concatenate(
+            lax.all_to_all(
+                jnp.stack([weights] * lax.axis_size(("range", "doppler"))),
+                ("range", "doppler"),
+                0,
+                0,
+            ),
+            axis=0,
+        ),
         preferred_element_type=jnp.float32,
     ).astype(jnp.bfloat16)
 

time: 432 us -> 616 us (1.43)
  blocking collectives: 0 us -> 303 us
  waiting for transfers between devices: 262 us -> 151 us
  between operations: 16.2 us -> 2.82 us
  local copies, waits for them, and re-layouts: 18.2 us -> 24.8 us
    all_to_all x0 -> x1, blocking collectives: none -> 303 us  [body(): lax.all_to_all(jnp.stack([weights] * lax.axis_size(('range', 'doppler')))...]
    all_gather x1 -> x0, waiting for transfers between devices: 111 us -> none  [body(): lax.all_gather(weights, ('range', 'doppler'), axis=0, tiled=True)]
    another operation x9 -> x10, local copies, waits for them, and re-layouts: 6.04 us -> 12.4 us  [the longest x1 6.37 us: body(): jnp.stack([weights] * lax.axis_size(('range', 'doppler')))]
  transfers between devices with their start and end apart: 2 -> 1, of which waited for: 2 -> 1; matrix products, arithmetic and copies ran while one was open for 0% -> 0% of each run, Pallas kernels for 0% -> 0%
where the time goes in v1:
time: 616 us
  blocking collectives  303 us (49%)
  waiting for transfers between devices  151 us (25%)
  other arithmetic  86.3 us (14%)
  matrix products  35.9 us (6%)
  local copies, waits for them, and re-layouts  24.8 us (4%)
  starting transfers between devices  11.9 us (2%)
    all_to_all x1, blocking collectives, body(): lax.all_to_all(jnp.stack([weights] * lax.axis_size(('range', 'doppler')))...  303 us
    all_to_all x1, waiting for transfers between devices, body(): lax.all_to_all(outgoing, ('range', 'doppler'), split_axis=0, concat_axis=...  151 us
    another operation x10, other arithmetic, adapt(): factor = jnp.linalg.cholesky(covariance)  56.4 us
    another operation x3, other arithmetic, solve_one(): lax.linalg.triangular_solve(factor, inner, left_side=True, lower=True, tr...  29.5 us
    dot_general x1, matrix products, body(): jnp.einsum('bgd,bde->bge', snapshots, jnp.concatenate(lax.all_to_all(jnp....  17.8 us
    dot_general x1, matrix products, adapt(): jnp.einsum('bnrd,bnre->bde', masked, blocks, preferred_element_type=jnp.f...  14.2 us
  transfers between devices with their start and end apart: 1, of which 1 were waited for; matrix products, arithmetic and copies ran while one was open for 0% of the time, Pallas kernels for 0%

profile of v1, /device:TPU:1, one launch (start us, length us, event | category | flops | bytes accessed | tf_op | source)
XLA Modules:
  0.0 615.6 jit_solution(15330382236924793743)
XLA Ops:
  0.0 11.9 %all-to-all-start = ((bf16[128,1,128,384]{3,2,1,0:T(8,128)(2,1)}), bf16[128,1,128,384]{3,2,1,0:T(8,128)(2,1)}, u32[]{:S(2)}, u32[]{:S(2)}) async-start(bf16[128,1,128,384]{3,2,1,0:T(8,128)(2,1)} %bitcast.156), calls=%async_computation | async-start | bytes 25165824 | tf_op jit(solution)/shard_map/all_to_all | solution.py:46
  12.8 150.7 %all-to-all-done = bf16[128,1,128,384]{3,2,1,0:T(8,128)(2,1)} async-done(((bf16[128,1,128,384]{3,2,1,0:T(8,128)(2,1)}), bf16[128,1,128,384]{3,2,1,0:T(8,128)(2,1)}, u32[]{:S(2)}, u32[]{:S(2)}) %all-to-all-start) | async-done | bytes 12582944 | tf_op jit(solution)/shard_map/all_to_all | solution.py:46
  163.5 14.2 %fusion.26 = f32[384,384]{0,1:T(8,128)S(1)} fusion(bf16[128,1,128,384]{3,2,1,0:T(8,128)(2,1)} %all-to-all-done, bf16[128]{0:T(256)(128)(2,1)S(1)} %convert_element_type.44, f32[]{:T(128)} %bitcast.6), kind=kOutput, calls=%fused_computation.26 | convolution fusion | flops 4838719488 | bytes 13172996 | tf_op jit(solution)/shard_map/bnrd,bnre->bde/dot_general | solution.py:29
  178.0 11.7 %custom-call.27 = f32[1,128,128]{2,1,0:T(8,128)S(1)} custom-call(f32[1,128,128]{2,1,0:T(8,128)S(1)} %cholesky.192), custom_call_target="Cholesky" | custom-call | tf_op jit(solution)/shard_map/jit(cholesky)/cholesky | solution.py:34
  189.7 9.8 %custom-call.28 = f32[1,1,128,128]{2,3,1,0:T(8,128)S(1)} custom-call(f32[1,1,128,128]{3,2,1,0:T(8,128)S(1)} %get-tuple-element.29), custom_call_target="InvertDiagBlocksLowerTriangular" | custom-call | tf_op jit(solution)/shard_map/jit(cholesky)/cholesky | solution.py:34
  200.2 11.7 %custom-call.29 = f32[1,128,128]{2,1,0:T(8,128)S(1)} custom-call(f32[1,128,128]{2,1,0:T(8,128)S(1)} %cholesky.196), custom_call_target="Cholesky" | custom-call | tf_op jit(solution)/shard_map/jit(cholesky)/cholesky | solution.py:34
  211.9 10.0 %custom-call.30 = f32[1,1,128,128]{2,3,1,0:T(8,128)S(1)} custom-call(f32[1,1,128,128]{3,2,1,0:T(8,128)S(1)} %get-tuple-element.26), custom_call_target="InvertDiagBlocksLowerTriangular" | custom-call | tf_op jit(solution)/shard_map/jit(cholesky)/cholesky | solution.py:34
  222.4 11.7 %custom-call.31 = f32[1,128,128]{2,1,0:T(8,128)S(1)} custom-call(f32[1,128,128]{2,1,0:T(8,128)S(1)} %fusion.20), custom_call_target="Cholesky" | custom-call | tf_op jit(solution)/shard_map/jit(cholesky)/cholesky | solution.py:34
  234.2 0.7 compare_reduce_fusion
  234.9 0.7 compare_reduce_fusion.1
  237.5 6.1 while.1
  237.6 0.6 fusion.63
  238.2 1.3 bitcast_dynamic-update-slice_fusion.2
  239.6 0.6 fusion.63
  240.2 1.3 bitcast_dynamic-update-slice_fusion.2
  241.7 0.6 fusion.63
  242.3 1.3 bitcast_dynamic-update-slice_fusion.2
  243.6 29.5 %custom-call.32 = f32[1,3,128,128]{2,3,1,0:T(8,128)S(1)} custom-call(f32[1,3,128,128]{3,2,1,0:T(8,128)S(1)} %bitcast.166), custom_call_target="InvertDiagBlocksLowerTriangular" | custom-call | tf_op jit(solution)/shard_map/vmap()/triangular_solve | solution.py:20
  274.8 0.3 convolution_subtract_fusion.1
  275.4 0.4 convolution_subtract_fusion
  276.4 6.4 %stack.2 = bf16[128,1,384,256]{2,3,1,0:T(8,128)(2,1)S(1)} broadcast(bf16[384,256]{0,1:T(8,128)(2,1)S(1)} %copy.18), dimensions={2,3} | broadcast | bytes 25362432 | tf_op jit(solution)/shard_map/stack | solution.py:56
  282.8 303.1 %all_to_all.10 = bf16[128,1,384,256]{2,3,1,0:T(8,128)(2,1)} all-to-all(bf16[128,1,384,256]{2,3,1,0:T(8,128)(2,1)S(1)} %stack.2), channel_id=1, replica_groups=mesh['range'=16,'doppler'=8] {'range','doppler'}, dimensions={0} | all-to-all | bytes 50331648 | tf_op jit(solution)/shard_map/all_to_all | solution.py:55
  585.9 17.8 %convert_bitcast_fusion = bf16[128,128,256]{1,2,0:T(8,128)(2,1)} fusion(bf16[128,128,384]{2,1,0:T(8,128)(2,1)} %param.4, bf16[128,1,384,256]{2,3,1,0:T(8,128)(2,1)} %all_to_all.10), kind=kOutput, calls=%fused_computation.8 | convolution fusion | flops 3225419776 | bytes 46137344 | tf_op jit(solution)/shard_map/bgd,bde->bge/dot_general | solution.py:51
  603.7 11.9 %copy.19 = bf16[128,128,256]{2,1,0:T(8,128)(2,1)} copy(bf16[128,128,256]{1,2,0:T(8,128)(2,1)} %convert_bitcast_fusion) | data formatting | bytes 16777216 | tf_op jit(solution)/shard_map/convert_element_type | solution.py:64
  (38 shorter events, 4.4 us)
Async XLA Ops:
  0.0 12.6 %copy-start.1 = (s32[1,128]{1,0:T(1,128)S(1)}, s32[1,128]{1,0:T(1,128)}, u32[]{:S(2)}) copy-start(s32[1,128]{1,0:T(1,128)} %param.6) | copy-start | bytes 1540
  0.0 12.7 %copy-start = (bf16[1,384,256]{2,1,0:T(8,128)(2,1)S(1)}, bf16[1,384,256]{2,1,0:T(8,128)(2,1)}, u32[]{:S(2)}) copy-start(bf16[1,384,256]{2,1,0:T(8,128)(2,1)} %param.5) | copy-start | bytes 589828
  0.0 163.5 %all-to-all-start = ((bf16[128,1,128,384]{3,2,1,0:T(8,128)(2,1)}), bf16[128,1,128,384]{3,2,1,0:T(8,128)(2,1)}, u32[]{:S(2)}, u32[]{:S(2)}) async-start(bf16[128,1,128,384]{3,2,1,0:T(8,128)(2,1)} %bitcast.156), calls=%async_computation | async-start | bytes 25165824 | tf_op jit(solution)/shard_map/all_to_all | solution.py:46
